TPU v7x, 32 devices: a whole 2x2x4 slice. The times are simulated.
32 devices in a mesh: level: 8 (over y, x, core), row: 4 (over z).
Axes of the slice: x: 2, y: 2, z: 4, core: 2. Of those that a mesh axis runs over, the one named last changes fastest.
Arguments:
- right_side: float32 [64, 32, 128], P('level'), may hold values from -6 to 6
- inverses: float32 [64, 128, 128], P('level'), as said below
- blocks: float32 [64, 8, 128, 128], P('level', 'row'), may hold values from -0.125 to 0.125
- sources: int32 [64, 8], P('level', 'row'), may hold values from -1 to 55, as said below
Outputs:
- solved: float32 [64, 32, 128], P('level')
Inputs may be any that keep to these rules, and one draw needn't show every extreme that they name: `sources`: the supernodes form an elimination tree: every supernode below the top level has one parent on the next level, and every supernode above level 0 has exactly one child. The entries of supernode t are its 8 highest-numbered descendants in that tree, distinct and in falling order, followed by -1 for empty slots; the supernodes of level 0 have only empty slots. `inverses`: lower triangular.
All inputs are finite; a program needn't handle non-finite values.
Results may differ from a plain program's by a relative error of at most 0.0001.
Values sent between devices are 32-bit elements; how exact they have to be, the bound alone decides.
No kernel may reach another device: no remote copies, remote signals or barrier semaphores. Data moves between devices by JAX's collectives and lax.ppermute only.
A program may use at most 64 MiB of HBM per device.

v0:
```python
import jax
import jax.numpy as jnp
from jax import lax
from jax.sharding import PartitionSpec as P


def spread(value, axis, source):
    kept = jnp.where(lax.axis_index(axis) == source, value, 0).astype(value.dtype)
    return lax.psum(kept, axis)


def per_device(right_side, inverses, blocks, sources):
    highest = lax.Precision.HIGHEST
    sn_count = right_side.shape[0]
    my_level = lax.axis_index("level")
    levels = lax.axis_size("level")

    def advance(level_now, carry):
        updates, solved = carry
        mine = my_level == level_now
        totals = lax.psum(updates, "row")
        own = jnp.einsum("snw,svw->snv", right_side - totals, inverses, precision=highest)
        current = spread(own, "level", level_now)
        solved = jnp.where(mine, current, solved)
        wanted = level_now * sn_count + jnp.arange(sn_count, dtype=jnp.int32)
        select = (sources[:, :, None] == wanted[None, None, :]).astype(jnp.float32)
        picked = jnp.einsum("srk,knw->srnw", select, current, precision=highest)
        updates = updates + jnp.einsum("srnw,srwv->snv", picked, blocks, precision=highest)
        return (updates, solved)

    empty = jnp.zeros(right_side.shape, jnp.float32)
    updates, solved = lax.fori_loop(0, levels, advance, (empty, empty))
    return solved


def solution(mesh):
    return jax.shard_map(
        per_device,
        mesh=mesh,
        in_specs=(
            P("level", None, None),
            P("level", None, None),
            P("level", "row", None, None),
            P("level", "row"),
        ),
        out_specs=P("level", None, None),
        check_vma=False,
    )
```

profile of v0, /device:TPU:0, one launch (start us, length us, event | category | flops | bytes accessed | tf_op | source)
XLA Modules:
  0.0 781.4 jit_solution(18321583379033328239)
XLA Ops:
  7.2 766.9 %while.18 = (s32[]{:T(128)}, f32[8,32,128]{2,1,0:T(8,128)S(1)}, f32[8,32,128]{2,1,0:T(8,128)S(1)}, s32[8,2]{0,1:T(2,128)S(1)}, f32[8,32,128]{2,1,0:T(8,128)}, /*...) while((s32[]{:T(128)}, f32[8,32,128]{2,1,0:T(8,128)S(1)}, ...), condition=%wide.region_3.4_spmd.clone, body=%wide.region_0.3_spmd.clone.sunk | while | flops 157548688 | bytes 10355576 | solution.py:32
  8.1 39.7 %all-reduce.3.cloned.1.call-done = f32[8,32,128]{2,1,0:T(8,128)} async-done(((f32[8,32,128]{2,1,0:T(8,128)}), f32[8,32,128]{2,1,0:T(8,128)}) %all-reduce.3.cloned.1.call-update) | async-done | bytes 131088 | tf_op jit(solution)/shard_map/while/body/eval_jaxpr/psum | solution.py:21
  47.7 2.8 convolution_select_fusion.2
  50.6 53.3 %all-reduce.5.cloned.1.call-done = f32[8,32,128]{2,1,0:T(8,128)} async-done(((f32[8,32,128]{2,1,0:T(8,128)}), f32[8,32,128]{2,1,0:T(8,128)}) %all-reduce.5.cloned.1.call-update) | async-done | bytes 131088 | tf_op jit(solution)/shard_map/while/body/eval_jaxpr/psum | solution.py:9
  107.1 36.3 %all-reduce.3.cloned.1.call-done = f32[8,32,128]{2,1,0:T(8,128)} async-done(((f32[8,32,128]{2,1,0:T(8,128)}), f32[8,32,128]{2,1,0:T(8,128)}) %all-reduce.3.cloned.1.call-update) | async-done | bytes 131088 | tf_op jit(solution)/shard_map/while/body/eval_jaxpr/psum | solution.py:21
  143.4 2.8 convolution_select_fusion.2
  146.2 53.2 %all-reduce.5.cloned.1.call-done = f32[8,32,128]{2,1,0:T(8,128)} async-done(((f32[8,32,128]{2,1,0:T(8,128)}), f32[8,32,128]{2,1,0:T(8,128)}) %all-reduce.5.cloned.1.call-update) | async-done | bytes 131088 | tf_op jit(solution)/shard_map/while/body/eval_jaxpr/psum | solution.py:9
  202.6 36.0 %all-reduce.3.cloned.1.call-done = f32[8,32,128]{2,1,0:T(8,128)} async-done(((f32[8,32,128]{2,1,0:T(8,128)}), f32[8,32,128]{2,1,0:T(8,128)}) %all-reduce.3.cloned.1.call-update) | async-done | bytes 131088 | tf_op jit(solution)/shard_map/while/body/eval_jaxpr/psum | solution.py:21
  238.6 2.8 convolution_select_fusion.2
  241.4 53.2 %all-reduce.5.cloned.1.call-done = f32[8,32,128]{2,1,0:T(8,128)} async-done(((f32[8,32,128]{2,1,0:T(8,128)}), f32[8,32,128]{2,1,0:T(8,128)}) %all-reduce.5.cloned.1.call-update) | async-done | bytes 131088 | tf_op jit(solution)/shard_map/while/body/eval_jaxpr/psum | solution.py:9
  297.8 36.3 %all-reduce.3.cloned.1.call-done = f32[8,32,128]{2,1,0:T(8,128)} async-done(((f32[8,32,128]{2,1,0:T(8,128)}), f32[8,32,128]{2,1,0:T(8,128)}) %all-reduce.3.cloned.1.call-update) | async-done | bytes 131088 | tf_op jit(solution)/shard_map/while/body/eval_jaxpr/psum | solution.py:21
  334.1 2.8 convolution_select_fusion.2
  336.9 53.3 %all-reduce.5.cloned.1.call-done = f32[8,32,128]{2,1,0:T(8,128)} async-done(((f32[8,32,128]{2,1,0:T(8,128)}), f32[8,32,128]{2,1,0:T(8,128)}) %all-reduce.5.cloned.1.call-update) | async-done | bytes 131088 | tf_op jit(solution)/shard_map/while/body/eval_jaxpr/psum | solution.py:9
  393.4 36.3 %all-reduce.3.cloned.1.call-done = f32[8,32,128]{2,1,0:T(8,128)} async-done(((f32[8,32,128]{2,1,0:T(8,128)}), f32[8,32,128]{2,1,0:T(8,128)}) %all-reduce.3.cloned.1.call-update) | async-done | bytes 131088 | tf_op jit(solution)/shard_map/while/body/eval_jaxpr/psum | solution.py:21
  429.7 2.8 convolution_select_fusion.2
  432.5 53.2 %all-reduce.5.cloned.1.call-done = f32[8,32,128]{2,1,0:T(8,128)} async-done(((f32[8,32,128]{2,1,0:T(8,128)}), f32[8,32,128]{2,1,0:T(8,128)}) %all-reduce.5.cloned.1.call-update) | async-done | bytes 131088 | tf_op jit(solution)/shard_map/while/body/eval_jaxpr/psum | solution.py:9
  488.9 36.3 %all-reduce.3.cloned.1.call-done = f32[8,32,128]{2,1,0:T(8,128)} async-done(((f32[8,32,128]{2,1,0:T(8,128)}), f32[8,32,128]{2,1,0:T(8,128)}) %all-reduce.3.cloned.1.call-update) | async-done | bytes 131088 | tf_op jit(solution)/shard_map/while/body/eval_jaxpr/psum | solution.py:21
  528.0 53.2 %all-reduce.5.cloned.1.call-done = f32[8,32,128]{2,1,0:T(8,128)} async-done(((f32[8,32,128]{2,1,0:T(8,128)}), f32[8,32,128]{2,1,0:T(8,128)}) %all-reduce.5.cloned.1.call-update) | async-done | bytes 131088 | tf_op jit(solution)/shard_map/while/body/eval_jaxpr/psum | solution.py:9
  584.4 36.3 %all-reduce.3.cloned.1.call-done = f32[8,32,128]{2,1,0:T(8,128)} async-done(((f32[8,32,128]{2,1,0:T(8,128)}), f32[8,32,128]{2,1,0:T(8,128)}) %all-reduce.3.cloned.1.call-update) | async-done | bytes 131088 | tf_op jit(solution)/shard_map/while/body/eval_jaxpr/psum | solution.py:21
  620.7 2.8 convolution_select_fusion.2
  623.5 53.2 %all-reduce.5.cloned.1.call-done = f32[8,32,128]{2,1,0:T(8,128)} async-done(((f32[8,32,128]{2,1,0:T(8,128)}), f32[8,32,128]{2,1,0:T(8,128)}) %all-reduce.5.cloned.1.call-update) | async-done | bytes 131088 | tf_op jit(solution)/shard_map/while/body/eval_jaxpr/psum | solution.py:9
  679.9 36.0 %all-reduce.3.cloned.1.call-done = f32[8,32,128]{2,1,0:T(8,128)} async-done(((f32[8,32,128]{2,1,0:T(8,128)}), f32[8,32,128]{2,1,0:T(8,128)}) %all-reduce.3.cloned.1.call-update) | async-done | bytes 131088 | tf_op jit(solution)/shard_map/while/body/eval_jaxpr/psum | solution.py:21
  715.9 2.8 convolution_select_fusion.2
  718.7 53.2 %all-reduce.5.cloned.1.call-done = f32[8,32,128]{2,1,0:T(8,128)} async-done(((f32[8,32,128]{2,1,0:T(8,128)}), f32[8,32,128]{2,1,0:T(8,128)}) %all-reduce.5.cloned.1.call-update) | async-done | bytes 131088 | tf_op jit(solution)/shard_map/while/body/eval_jaxpr/psum | solution.py:9
  (143 shorter events, 29.0 us)
Async XLA Ops:
  7.2 98.0 %copy-start.1 = (f32[8,2,128,128]{3,2,1,0:T(8,128)S(1)}, f32[8,2,128,128]{3,2,1,0:T(8,128)}, u32[]{:S(2)}) copy-start(f32[8,2,128,128]{3,2,1,0:T(8,128)} %get-tuple-element.328) | copy-start | bytes 3145732 | tf_op jit(solution)/shard_map/while
  7.2 40.5 %all-reduce.3.cloned.1.call-start = ((), (), s32[]{:S(2)}) async-start(), calls=%async_computation | async-start | bytes 262144 | tf_op jit(solution)/shard_map/while/body/eval_jaxpr/psum | solution.py:21
  7.9 96.0 %all-reduce.5.cloned.1.call-start = ((), (), s32[]{:S(2)}) async-start(), calls=%async_computation.1 | async-start | bytes 262144 | tf_op jit(solution)/shard_map/while/body/eval_jaxpr/psum | solution.py:9
  106.2 94.5 %copy-start.1 = (f32[8,2,128,128]{3,2,1,0:T(8,128)S(1)}, f32[8,2,128,128]{3,2,1,0:T(8,128)}, u32[]{:S(2)}) copy-start(f32[8,2,128,128]{3,2,1,0:T(8,128)} %get-tuple-element.328) | copy-start | bytes 3145732 | tf_op jit(solution)/shard_map/while
  106.2 37.2 %all-reduce.3.cloned.1.call-start = ((), (), s32[]{:S(2)}) async-start(), calls=%async_computation | async-start | bytes 262144 | tf_op jit(solution)/shard_map/while/body/eval_jaxpr/psum | solution.py:21
  106.9 92.5 %all-reduce.5.cloned.1.call-start = ((), (), s32[]{:S(2)}) async-start(), calls=%async_computation.1 | async-start | bytes 262144 | tf_op jit(solution)/shard_map/while/body/eval_jaxpr/psum | solution.py:9
  201.7 94.2 %copy-start.1 = (f32[8,2,128,128]{3,2,1,0:T(8,128)S(1)}, f32[8,2,128,128]{3,2,1,0:T(8,128)}, u32[]{:S(2)}) copy-start(f32[8,2,128,128]{3,2,1,0:T(8,128)} %get-tuple-element.328) | copy-start | bytes 3145732 | tf_op jit(solution)/shard_map/while
  201.7 36.9 %all-reduce.3.cloned.1.call-start = ((), (), s32[]{:S(2)}) async-start(), calls=%async_computation | async-start | bytes 262144 | tf_op jit(solution)/shard_map/while/body/eval_jaxpr/psum | solution.py:21
  202.4 92.2 %all-reduce.5.cloned.1.call-start = ((), (), s32[]{:S(2)}) async-start(), calls=%async_computation.1 | async-start | bytes 262144 | tf_op jit(solution)/shard_map/while/body/eval_jaxpr/psum | solution.py:9
  296.9 94.7 %copy-start.1 = (f32[8,2,128,128]{3,2,1,0:T(8,128)S(1)}, f32[8,2,128,128]{3,2,1,0:T(8,128)}, u32[]{:S(2)}) copy-start(f32[8,2,128,128]{3,2,1,0:T(8,128)} %get-tuple-element.328) | copy-start | bytes 3145732 | tf_op jit(solution)/shard_map/while
  296.9 37.2 %all-reduce.3.cloned.1.call-start = ((), (), s32[]{:S(2)}) async-start(), calls=%async_computation | async-start | bytes 262144 | tf_op jit(solution)/shard_map/while/body/eval_jaxpr/psum | solution.py:21
  297.6 92.6 %all-reduce.5.cloned.1.call-start = ((), (), s32[]{:S(2)}) async-start(), calls=%async_computation.1 | async-start | bytes 262144 | tf_op jit(solution)/shard_map/while/body/eval_jaxpr/psum | solution.py:9
  392.5 94.5 %copy-start.1 = (f32[8,2,128,128]{3,2,1,0:T(8,128)S(1)}, f32[8,2,128,128]{3,2,1,0:T(8,128)}, u32[]{:S(2)}) copy-start(f32[8,2,128,128]{3,2,1,0:T(8,128)} %get-tuple-element.328) | copy-start | bytes 3145732 | tf_op jit(solution)/shard_map/while
  392.5 37.2 %all-reduce.3.cloned.1.call-start = ((), (), s32[]{:S(2)}) async-start(), calls=%async_computation | async-start | bytes 262144 | tf_op jit(solution)/shard_map/while/body/eval_jaxpr/psum | solution.py:21
  393.2 92.5 %all-reduce.5.cloned.1.call-start = ((), (), s32[]{:S(2)}) async-start(), calls=%async_computation.1 | async-start | bytes 262144 | tf_op jit(solution)/shard_map/while/body/eval_jaxpr/psum | solution.py:9
  488.0 94.5 %copy-start.1 = (f32[8,2,128,128]{3,2,1,0:T(8,128)S(1)}, f32[8,2,128,128]{3,2,1,0:T(8,128)}, u32[]{:S(2)}) copy-start(f32[8,2,128,128]{3,2,1,0:T(8,128)} %get-tuple-element.328) | copy-start | bytes 3145732 | tf_op jit(solution)/shard_map/while
  488.0 37.2 %all-reduce.3.cloned.1.call-start = ((), (), s32[]{:S(2)}) async-start(), calls=%async_computation | async-start | bytes 262144 | tf_op jit(solution)/shard_map/while/body/eval_jaxpr/psum | solution.py:21
  488.7 92.5 %all-reduce.5.cloned.1.call-start = ((), (), s32[]{:S(2)}) async-start(), calls=%async_computation.1 | async-start | bytes 262144 | tf_op jit(solution)/shard_map/while/body/eval_jaxpr/psum | solution.py:9
  583.5 94.5 %copy-start.1 = (f32[8,2,128,128]{3,2,1,0:T(8,128)S(1)}, f32[8,2,128,128]{3,2,1,0:T(8,128)}, u32[]{:S(2)}) copy-start(f32[8,2,128,128]{3,2,1,0:T(8,128)} %get-tuple-element.328) | copy-start | bytes 3145732 | tf_op jit(solution)/shard_map/while
  583.5 37.2 %all-reduce.3.cloned.1.call-start = ((), (), s32[]{:S(2)}) async-start(), calls=%async_computation | async-start | bytes 262144 | tf_op jit(solution)/shard_map/while/body/eval_jaxpr/psum | solution.py:21
  584.2 92.5 %all-reduce.5.cloned.1.call-start = ((), (), s32[]{:S(2)}) async-start(), calls=%async_computation.1 | async-start | bytes 262144 | tf_op jit(solution)/shard_map/while/body/eval_jaxpr/psum | solution.py:9
  679.0 94.2 %copy-start.1 = (f32[8,2,128,128]{3,2,1,0:T(8,128)S(1)}, f32[8,2,128,128]{3,2,1,0:T(8,128)}, u32[]{:S(2)}) copy-start(f32[8,2,128,128]{3,2,1,0:T(8,128)} %get-tuple-element.328) | copy-start | bytes 3145732 | tf_op jit(solution)/shard_map/while
  679.0 36.9 %all-reduce.3.cloned.1.call-start = ((), (), s32[]{:S(2)}) async-start(), calls=%async_computation | async-start | bytes 262144 | tf_op jit(solution)/shard_map/while/body/eval_jaxpr/psum | solution.py:21
  679.7 92.2 %all-reduce.5.cloned.1.call-start = ((), (), s32[]{:S(2)}) async-start(), calls=%async_computation.1 | async-start | bytes 262144 | tf_op jit(solution)/shard_map/while/body/eval_jaxpr/psum | solution.py:9
  (18 other events, 18.6 us)
Sparse Core Ops, SparseCore 0:
  10.3 37.3 all-reduce.2
  50.8 53.1 all-reduce.4
  109.3 34.0 all-reduce.2
  146.3 53.1 all-reduce.4
  204.5 34.0 all-reduce.2
  241.5 53.1 all-reduce.4
  300.0 34.0 all-reduce.2
  337.1 53.1 all-reduce.4
  395.6 34.0 all-reduce.2
  432.6 53.1 all-reduce.4
  491.1 34.0 all-reduce.2
  528.1 53.1 all-reduce.4
  586.6 34.0 all-reduce.2
  623.6 53.1 all-reduce.4
  681.8 34.0 all-reduce.2
  718.8 53.1 all-reduce.4
where the time goes:
time: 782 us; the launch traced here: 781 us
  waiting for transfers between devices  719 us (92%)
  matrix products  37.5 us (5%)
  between operations  13.1 us (2%)
    psum x8, waiting for transfers between devices, spread(): return lax.psum(kept, axis)  426 us
    psum x8, waiting for transfers between devices, advance(): totals = lax.psum(updates, 'row')  293 us
    dot_general x8, matrix products, advance(): jnp.einsum('snw,svw->snv', right_side - totals, inverses, precision=highest)  22 us
  transfers between devices with their start and end apart: 16, of which 16 were waited for; matrix products, arithmetic and copies ran while one was open for 0% of the time, Pallas kernels for 0%

commit v1 on v0

--- a/solution.py
+++ b/solution.py
@@ -18,7 +18,7 @@
     def advance(level_now, carry):
         updates, solved = carry
         mine = my_level == level_now
-        totals = lax.psum(updates, "row")
+        totals = jnp.sum(lax.all_gather(updates, "row"), axis=0)
         own = jnp.einsum("snw,svw->snv", right_side - totals, inverses, precision=highest)
         current = spread(own, "level", level_now)
         solved = jnp.where(mine, current, solved)

time: 782 us -> 602 us (0.77)
  waiting for transfers between devices: 719 us -> 432 us
  blocking collectives: 0 us -> 123 us
  matrix products: 37.5 us -> 28 us
    psum x8 -> x0, waiting for transfers between devices: 293 us -> none  [advance(): totals = lax.psum(updates, 'row')]
    all_gather x0 -> x8, blocking collectives: none -> 123 us  [advance(): totals = jnp.sum(lax.all_gather(updates, 'row'), axis=0)]
    dot_general x8, matrix products: 22 us -> 12.7 us  [advance(): jnp.einsum('snw,svw->snv', right_side - totals, inverses, precision=highest)]
  transfers between devices with their start and end apart: 16 -> 8, of which waited for: 16 -> 8; matrix products, arithmetic and copies ran while one was open for 0% -> 0% of each run, Pallas kernels for 0% -> 0%
where the time goes in v1:
time: 602 us; the launch traced here: 601 us
  waiting for transfers between devices  432 us (72%)
  blocking collectives  123 us (20%)
  matrix products  28 us (5%)
  between operations  13.4 us (2%)
    psum x8, waiting for transfers between devices, spread(): return lax.psum(kept, axis)  432 us
    all_gather x8, blocking collectives, advance(): totals = jnp.sum(lax.all_gather(updates, 'row'), axis=0)  123 us
    dot_general x8, matrix products, advance(): jnp.einsum('snw,svw->snv', right_side - totals, inverses, precision=highest)  12.7 us
  transfers between devices with their start and end apart: 8, of which 8 were waited for; matrix products, arithmetic and copies ran while one was open for 0% of the time, Pallas kernels for 0%

profile of v1, /device:TPU:0, one launch (start us, length us, event | category | flops | bytes accessed | tf_op | source)
XLA Modules:
  0.0 601.1 jit_solution(16876373846883631647)
XLA Ops:
  7.2 586.4 %while.18 = (s32[]{:T(128)}, f32[8,32,128]{2,1,0:T(8,128)S(1)}, f32[8,32,128]{2,1,0:T(8,128)S(1)}, s32[8,2]{0,1:T(2,128)S(1)}, f32[8,32,128]{2,1,0:T(8,128)}, /*...) while((s32[]{:T(128)}, f32[8,32,128]{2,1,0:T(8,128)S(1)}, ...), condition=%wide.region_3.4_spmd.clone, body=%wide.region_0.3_spmd.clone.sunk | while | flops 157614224 | bytes 12976624 | solution.py:32
  7.3 17.5 %all-gather.3 = f32[32,32,128]{2,1,0:T(8,128)S(1)} all-gather(f32[8,32,128]{2,1,0:T(8,128)S(1)} %broadcast_select_fusion.2), channel_id=2, replica_groups=mesh['level'=8,'row'=4] {'row'}, dimensions={0}, use_global_device_ids=true | all-gather | bytes 655360 | tf_op jit(solution)/shard_map/while/body/eval_jaxpr/all_gather | solution.py:21
  24.8 1.6 convolution_select_fusion.2
  26.5 55.3 %all-reduce.2.cloned.1.call-done = f32[8,32,128]{2,1,0:T(8,128)} async-done(((f32[8,32,128]{2,1,0:T(8,128)}), f32[8,32,128]{2,1,0:T(8,128)}) %all-reduce.2.cloned.1.call-update) | async-done | bytes 131088 | tf_op jit(solution)/shard_map/while/body/eval_jaxpr/psum | solution.py:9
  84.1 15.1 %all-gather.3 = f32[32,32,128]{2,1,0:T(8,128)S(1)} all-gather(f32[8,32,128]{2,1,0:T(8,128)S(1)} %broadcast_select_fusion.2), channel_id=2, replica_groups=mesh['level'=8,'row'=4] {'row'}, dimensions={0}, use_global_device_ids=true | all-gather | bytes 655360 | tf_op jit(solution)/shard_map/while/body/eval_jaxpr/all_gather | solution.py:21
  99.2 1.6 convolution_select_fusion.2
  100.8 53.7 %all-reduce.2.cloned.1.call-done = f32[8,32,128]{2,1,0:T(8,128)} async-done(((f32[8,32,128]{2,1,0:T(8,128)}), f32[8,32,128]{2,1,0:T(8,128)}) %all-reduce.2.cloned.1.call-update) | async-done | bytes 131088 | tf_op jit(solution)/shard_map/while/body/eval_jaxpr/psum | solution.py:9
  156.9 15.1 %all-gather.3 = f32[32,32,128]{2,1,0:T(8,128)S(1)} all-gather(f32[8,32,128]{2,1,0:T(8,128)S(1)} %broadcast_select_fusion.2), channel_id=2, replica_groups=mesh['level'=8,'row'=4] {'row'}, dimensions={0}, use_global_device_ids=true | all-gather | bytes 655360 | tf_op jit(solution)/shard_map/while/body/eval_jaxpr/all_gather | solution.py:21
  172.0 1.6 convolution_select_fusion.2
  173.6 53.7 %all-reduce.2.cloned.1.call-done = f32[8,32,128]{2,1,0:T(8,128)} async-done(((f32[8,32,128]{2,1,0:T(8,128)}), f32[8,32,128]{2,1,0:T(8,128)}) %all-reduce.2.cloned.1.call-update) | async-done | bytes 131088 | tf_op jit(solution)/shard_map/while/body/eval_jaxpr/psum | solution.py:9
  229.7 15.1 %all-gather.3 = f32[32,32,128]{2,1,0:T(8,128)S(1)} all-gather(f32[8,32,128]{2,1,0:T(8,128)S(1)} %broadcast_select_fusion.2), channel_id=2, replica_groups=mesh['level'=8,'row'=4] {'row'}, dimensions={0}, use_global_device_ids=true | all-gather | bytes 655360 | tf_op jit(solution)/shard_map/while/body/eval_jaxpr/all_gather | solution.py:21
  244.8 1.6 convolution_select_fusion.2
  246.4 53.7 %all-reduce.2.cloned.1.call-done = f32[8,32,128]{2,1,0:T(8,128)} async-done(((f32[8,32,128]{2,1,0:T(8,128)}), f32[8,32,128]{2,1,0:T(8,128)}) %all-reduce.2.cloned.1.call-update) | async-done | bytes 131088 | tf_op jit(solution)/shard_map/while/body/eval_jaxpr/psum | solution.py:9
  302.5 15.1 %all-gather.3 = f32[32,32,128]{2,1,0:T(8,128)S(1)} all-gather(f32[8,32,128]{2,1,0:T(8,128)S(1)} %broadcast_select_fusion.2), channel_id=2, replica_groups=mesh['level'=8,'row'=4] {'row'}, dimensions={0}, use_global_device_ids=true | all-gather | bytes 655360 | tf_op jit(solution)/shard_map/while/body/eval_jaxpr/all_gather | solution.py:21
  317.6 1.6 convolution_select_fusion.2
  319.2 53.8 %all-reduce.2.cloned.1.call-done = f32[8,32,128]{2,1,0:T(8,128)} async-done(((f32[8,32,128]{2,1,0:T(8,128)}), f32[8,32,128]{2,1,0:T(8,128)}) %all-reduce.2.cloned.1.call-update) | async-done | bytes 131088 | tf_op jit(solution)/shard_map/while/body/eval_jaxpr/psum | solution.py:9
  375.3 15.1 %all-gather.3 = f32[32,32,128]{2,1,0:T(8,128)S(1)} all-gather(f32[8,32,128]{2,1,0:T(8,128)S(1)} %broadcast_select_fusion.2), channel_id=2, replica_groups=mesh['level'=8,'row'=4] {'row'}, dimensions={0}, use_global_device_ids=true | all-gather | bytes 655360 | tf_op jit(solution)/shard_map/while/body/eval_jaxpr/all_gather | solution.py:21
  390.4 1.6 convolution_select_fusion.2
  392.1 53.7 %all-reduce.2.cloned.1.call-done = f32[8,32,128]{2,1,0:T(8,128)} async-done(((f32[8,32,128]{2,1,0:T(8,128)}), f32[8,32,128]{2,1,0:T(8,128)}) %all-reduce.2.cloned.1.call-update) | async-done | bytes 131088 | tf_op jit(solution)/shard_map/while/body/eval_jaxpr/psum | solution.py:9
  448.1 15.1 %all-gather.3 = f32[32,32,128]{2,1,0:T(8,128)S(1)} all-gather(f32[8,32,128]{2,1,0:T(8,128)S(1)} %broadcast_select_fusion.2), channel_id=2, replica_groups=mesh['level'=8,'row'=4] {'row'}, dimensions={0}, use_global_device_ids=true | all-gather | bytes 655360 | tf_op jit(solution)/shard_map/while/body/eval_jaxpr/all_gather | solution.py:21
  463.2 1.6 convolution_select_fusion.2
  464.8 53.8 %all-reduce.2.cloned.1.call-done = f32[8,32,128]{2,1,0:T(8,128)} async-done(((f32[8,32,128]{2,1,0:T(8,128)}), f32[8,32,128]{2,1,0:T(8,128)}) %all-reduce.2.cloned.1.call-update) | async-done | bytes 131088 | tf_op jit(solution)/shard_map/while/body/eval_jaxpr/psum | solution.py:9
  520.9 15.1 %all-gather.3 = f32[32,32,128]{2,1,0:T(8,128)S(1)} all-gather(f32[8,32,128]{2,1,0:T(8,128)S(1)} %broadcast_select_fusion.2), channel_id=2, replica_groups=mesh['level'=8,'row'=4] {'row'}, dimensions={0}, use_global_device_ids=true | all-gather | bytes 655360 | tf_op jit(solution)/shard_map/while/body/eval_jaxpr/all_gather | solution.py:21
  537.7 53.7 %all-reduce.2.cloned.1.call-done = f32[8,32,128]{2,1,0:T(8,128)} async-done(((f32[8,32,128]{2,1,0:T(8,128)}), f32[8,32,128]{2,1,0:T(8,128)}) %all-reduce.2.cloned.1.call-update) | async-done | bytes 131088 | tf_op jit(solution)/shard_map/while/body/eval_jaxpr/psum | solution.py:9
  (135 shorter events, 21.0 us)
Async XLA Ops:
  7.2 74.6 %all-reduce.2.cloned.1.call-start = ((), (), s32[]{:S(2)}) async-start(), calls=%async_computation | async-start | bytes 262144 | tf_op jit(solution)/shard_map/while/body/eval_jaxpr/psum | solution.py:9
  7.2 17.6 %copy-start.2 = (f32[8,128,128]{2,1,0:T(8,128)S(1)}, f32[8,128,128]{2,1,0:T(8,128)}, u32[]{:S(2)}) copy-start(f32[8,128,128]{2,1,0:T(8,128)} %get-tuple-element.329) | copy-start | bytes 1572868 | tf_op jit(solution)/shard_map/while
  7.2 17.6 %copy-start.3 = (f32[8,32,128]{2,1,0:T(8,128)S(1)}, f32[8,32,128]{2,1,0:T(8,128)}, u32[]{:S(2)}) copy-start(f32[8,32,128]{2,1,0:T(8,128)} %get-tuple-element.328) | copy-start | bytes 393220 | tf_op jit(solution)/shard_map/while
  24.8 58.2 %copy-start = (f32[8,2,128,128]{3,2,1,0:T(8,128)S(1)}, f32[8,2,128,128]{3,2,1,0:T(8,128)}, u32[]{:S(2)}) copy-start(f32[8,2,128,128]{3,2,1,0:T(8,128)} %get-tuple-element.330) | copy-start | bytes 3145732 | tf_op jit(solution)/shard_map/while
  84.0 70.6 %all-reduce.2.cloned.1.call-start = ((), (), s32[]{:S(2)}) async-start(), calls=%async_computation | async-start | bytes 262144 | tf_op jit(solution)/shard_map/while/body/eval_jaxpr/psum | solution.py:9
  84.1 15.1 %copy-start.2 = (f32[8,128,128]{2,1,0:T(8,128)S(1)}, f32[8,128,128]{2,1,0:T(8,128)}, u32[]{:S(2)}) copy-start(f32[8,128,128]{2,1,0:T(8,128)} %get-tuple-element.329) | copy-start | bytes 1572868 | tf_op jit(solution)/shard_map/while
  84.1 15.1 %copy-start.3 = (f32[8,32,128]{2,1,0:T(8,128)S(1)}, f32[8,32,128]{2,1,0:T(8,128)}, u32[]{:S(2)}) copy-start(f32[8,32,128]{2,1,0:T(8,128)} %get-tuple-element.328) | copy-start | bytes 393220 | tf_op jit(solution)/shard_map/while
  99.2 56.7 %copy-start = (f32[8,2,128,128]{3,2,1,0:T(8,128)S(1)}, f32[8,2,128,128]{3,2,1,0:T(8,128)}, u32[]{:S(2)}) copy-start(f32[8,2,128,128]{3,2,1,0:T(8,128)} %get-tuple-element.330) | copy-start | bytes 3145732 | tf_op jit(solution)/shard_map/while
  156.8 70.6 %all-reduce.2.cloned.1.call-start = ((), (), s32[]{:S(2)}) async-start(), calls=%async_computation | async-start | bytes 262144 | tf_op jit(solution)/shard_map/while/body/eval_jaxpr/psum | solution.py:9
  156.9 15.1 %copy-start.2 = (f32[8,128,128]{2,1,0:T(8,128)S(1)}, f32[8,128,128]{2,1,0:T(8,128)}, u32[]{:S(2)}) copy-start(f32[8,128,128]{2,1,0:T(8,128)} %get-tuple-element.329) | copy-start | bytes 1572868 | tf_op jit(solution)/shard_map/while
  156.9 15.1 %copy-start.3 = (f32[8,32,128]{2,1,0:T(8,128)S(1)}, f32[8,32,128]{2,1,0:T(8,128)}, u32[]{:S(2)}) copy-start(f32[8,32,128]{2,1,0:T(8,128)} %get-tuple-element.328) | copy-start | bytes 393220 | tf_op jit(solution)/shard_map/while
  171.9 56.7 %copy-start = (f32[8,2,128,128]{3,2,1,0:T(8,128)S(1)}, f32[8,2,128,128]{3,2,1,0:T(8,128)}, u32[]{:S(2)}) copy-start(f32[8,2,128,128]{3,2,1,0:T(8,128)} %get-tuple-element.330) | copy-start | bytes 3145732 | tf_op jit(solution)/shard_map/while
  229.6 70.6 %all-reduce.2.cloned.1.call-start = ((), (), s32[]{:S(2)}) async-start(), calls=%async_computation | async-start | bytes 262144 | tf_op jit(solution)/shard_map/while/body/eval_jaxpr/psum | solution.py:9
  244.7 56.7 %copy-start = (f32[8,2,128,128]{3,2,1,0:T(8,128)S(1)}, f32[8,2,128,128]{3,2,1,0:T(8,128)}, u32[]{:S(2)}) copy-start(f32[8,2,128,128]{3,2,1,0:T(8,128)} %get-tuple-element.330) | copy-start | bytes 3145732 | tf_op jit(solution)/shard_map/while
  302.4 70.6 %all-reduce.2.cloned.1.call-start = ((), (), s32[]{:S(2)}) async-start(), calls=%async_computation | async-start | bytes 262144 | tf_op jit(solution)/shard_map/while/body/eval_jaxpr/psum | solution.py:9
  317.5 56.7 %copy-start = (f32[8,2,128,128]{3,2,1,0:T(8,128)S(1)}, f32[8,2,128,128]{3,2,1,0:T(8,128)}, u32[]{:S(2)}) copy-start(f32[8,2,128,128]{3,2,1,0:T(8,128)} %get-tuple-element.330) | copy-start | bytes 3145732 | tf_op jit(solution)/shard_map/while
  375.2 70.6 %all-reduce.2.cloned.1.call-start = ((), (), s32[]{:S(2)}) async-start(), calls=%async_computation | async-start | bytes 262144 | tf_op jit(solution)/shard_map/while/body/eval_jaxpr/psum | solution.py:9
  390.4 56.7 %copy-start = (f32[8,2,128,128]{3,2,1,0:T(8,128)S(1)}, f32[8,2,128,128]{3,2,1,0:T(8,128)}, u32[]{:S(2)}) copy-start(f32[8,2,128,128]{3,2,1,0:T(8,128)} %get-tuple-element.330) | copy-start | bytes 3145732 | tf_op jit(solution)/shard_map/while
  448.0 70.6 %all-reduce.2.cloned.1.call-start = ((), (), s32[]{:S(2)}) async-start(), calls=%async_computation | async-start | bytes 262144 | tf_op jit(solution)/shard_map/while/body/eval_jaxpr/psum | solution.py:9
  463.2 56.7 %copy-start = (f32[8,2,128,128]{3,2,1,0:T(8,128)S(1)}, f32[8,2,128,128]{3,2,1,0:T(8,128)}, u32[]{:S(2)}) copy-start(f32[8,2,128,128]{3,2,1,0:T(8,128)} %get-tuple-element.330) | copy-start | bytes 3145732 | tf_op jit(solution)/shard_map/while
  520.8 70.6 %all-reduce.2.cloned.1.call-start = ((), (), s32[]{:S(2)}) async-start(), calls=%async_computation | async-start | bytes 262144 | tf_op jit(solution)/shard_map/while/body/eval_jaxpr/psum | solution.py:9
  520.9 15.1 %copy-start.2 = (f32[8,128,128]{2,1,0:T(8,128)S(1)}, f32[8,128,128]{2,1,0:T(8,128)}, u32[]{:S(2)}) copy-start(f32[8,128,128]{2,1,0:T(8,128)} %get-tuple-element.329) | copy-start | bytes 1572868 | tf_op jit(solution)/shard_map/while
  520.9 15.1 %copy-start.3 = (f32[8,32,128]{2,1,0:T(8,128)S(1)}, f32[8,32,128]{2,1,0:T(8,128)}, u32[]{:S(2)}) copy-start(f32[8,32,128]{2,1,0:T(8,128)} %get-tuple-element.328) | copy-start | bytes 393220 | tf_op jit(solution)/shard_map/while
  536.0 56.7 %copy-start = (f32[8,2,128,128]{3,2,1,0:T(8,128)S(1)}, f32[8,2,128,128]{3,2,1,0:T(8,128)}, u32[]{:S(2)}) copy-start(f32[8,2,128,128]{3,2,1,0:T(8,128)} %get-tuple-element.330) | copy-start | bytes 3145732 | tf_op jit(solution)/shard_map/while
  (18 other events, 129.6 us)
Sparse Core Ops, SparseCore 0:
  26.6 55.1 all-reduce.1
  100.9 53.5 all-reduce.1
  173.7 53.5 all-reduce.1
  246.5 53.5 all-reduce.1
  319.3 53.6 all-reduce.1
  392.2 53.5 all-reduce.1
  464.9 53.6 all-reduce.1
  537.8 53.5 all-reduce.1
